TPU v7x, 512 devices: a whole 4x8x8 slice. The times are simulated.
512 devices in a mesh: seq: 64 (over x, z, core), head: 8 (over y).
Axes of the slice: x: 4, y: 8, z: 8, core: 2. Of those that a mesh axis runs over, the one named last changes fastest.
Arguments:
- queries: bfloat16 [32768, 4096], P(('seq', 'head'))
- key_vectors: bfloat16 [32768, 4096], P(('seq', 'head'))
- value_vectors: bfloat16 [32768, 4096], P(('seq', 'head')), may hold values from -6 to 6
- out_grads: bfloat16 [32768, 4096], P(('seq', 'head')), may hold values from -6 to 6
- extra_blocks: int32 [64, 8, 8], P('seq'), may hold values 0 or 1
- summary_rows: int32 [64, 16], P('seq'), may hold values from 0 to 511, as said below
Outputs:
- attention: bfloat16 [32768, 4096], P(('seq', 'head'))
- query_grad: bfloat16 [32768, 4096], P(('seq', 'head'))
- key_grad: bfloat16 [32768, 4096], P(('seq', 'head'))
- value_grad: bfloat16 [32768, 4096], P(('seq', 'head'))
Inputs may be any that keep to these rules, and one draw needn't show every extreme that they name: `summary_rows`: summary row s of a group lies in [s * 32, (s + 1) * 32), so the rows of a group are distinct and ascending.
All inputs are finite; a program needn't handle non-finite values. No bound on the sum of `extra_blocks` on one device may be relied on, other than what follows from the above.
Results may differ from a plain program's by a relative error of at most 0.022.
Values may be sent and summed in bfloat16 or wider, within the bound.
A program may use at most 64 MiB of HBM per device.

v0:
```python
import math

import jax
import jax.numpy as jnp
from jax import lax
from jax.sharding import PartitionSpec as P

HD = 128


neg_big = -1e30


def head_scores(query_heads, key_heads, factor):
    return (
        jnp.einsum("qhd,khd->hqk", query_heads, key_heads, preferred_element_type=jnp.float32)
        * factor
    )


def local_allowed(extra_map, group_len):
    block_count = extra_map.shape[0]
    block_len = group_len // block_count
    block_ids = jnp.arange(block_count, dtype=jnp.int32)
    block_lag = block_ids[:, None] - block_ids[None, :]
    allowed = (block_lag == 0) | (block_lag == 1) | (extra_map == 1) & (block_lag > 0)
    allowed = jnp.repeat(jnp.repeat(allowed, block_len, axis=0), block_len, axis=1)
    positions = jnp.arange(group_len, dtype=jnp.int32)
    return allowed & (positions[None, :] <= positions[:, None])


def key_window(summary_keys, summary_vals, block_id, key_rows, lower_end, upper_end, per_group):
    offset = block_id * key_rows
    key_block = lax.dynamic_slice_in_dim(summary_keys, offset, key_rows, 0)
    val_block = lax.dynamic_slice_in_dim(summary_vals, offset, key_rows, 0)
    owners = (offset + jnp.arange(key_rows, dtype=jnp.int32)) // per_group
    usable = (owners >= lower_end) & (owners < upper_end)
    return (offset, key_block, val_block, usable[None, None, :])


def block_bounds(lower_end, upper_end, key_rows, per_group):
    begin_block = lower_end * per_group // key_rows
    end_block = (upper_end * per_group + key_rows - 1) // key_rows
    return (begin_block, jnp.where(upper_end > lower_end, end_block, begin_block))


def softmax_stats(
    query_heads, summary_keys, summary_vals, lower_end, upper_end, key_rows, per_group, factor
):
    begin_block, end_block = block_bounds(lower_end, upper_end, key_rows, per_group)

    def softmax_advance(block_id, carried):
        peak, summed = carried
        offset, key_block, val_block, usable = key_window(
            summary_keys, summary_vals, block_id, key_rows, lower_end, upper_end, per_group
        )
        scores = jnp.where(usable, head_scores(query_heads, key_block, factor), neg_big)
        new_peak = jnp.maximum(peak, jnp.max(scores, axis=2))
        summed = summed * jnp.exp(peak - new_peak) + jnp.sum(
            jnp.exp(scores - new_peak[..., None]), axis=2
        )
        return (new_peak, summed)

    shape_hq = (query_heads.shape[1], query_heads.shape[0])
    start_stats = (jnp.full(shape_hq, neg_big, jnp.float32), jnp.zeros(shape_hq, jnp.float32))
    return lax.fori_loop(begin_block, end_block, softmax_advance, start_stats)


def merge_stats(earlier, later):
    peak = jnp.maximum(earlier[0], later[0])
    return (peak, earlier[1] * jnp.exp(earlier[0] - peak) + later[1] * jnp.exp(later[0] - peak))


def weighted_values(
    query_heads,
    log_mass,
    summary_keys,
    summary_vals,
    lower_end,
    upper_end,
    key_rows,
    per_group,
    factor,
):
    begin_block, end_block = block_bounds(lower_end, upper_end, key_rows, per_group)

    def weighted_advance(block_id, summed_values):
        offset, key_block, val_block, usable = key_window(
            summary_keys, summary_vals, block_id, key_rows, lower_end, upper_end, per_group
        )
        weights = jnp.where(
            usable, jnp.exp(head_scores(query_heads, key_block, factor) - log_mass[..., None]), 0.0
        ).astype(jnp.bfloat16)
        return summed_values + jnp.einsum(
            "hqk,khd->qhd", weights, val_block, preferred_element_type=jnp.float32
        )

    return lax.fori_loop(
        begin_block, end_block, weighted_advance, jnp.zeros(query_heads.shape, jnp.float32)
    )


def summary_backward(
    query_heads,
    grad_heads,
    log_mass,
    row_dot,
    summary_keys,
    summary_vals,
    lower_end,
    upper_end,
    key_rows,
    per_group,
    factor,
    carried,
):
    begin_block, end_block = block_bounds(lower_end, upper_end, key_rows, per_group)

    def summary_advance(block_id, running):
        query_acc, key_terms, val_terms = running
        offset, key_block, val_block, usable = key_window(
            summary_keys, summary_vals, block_id, key_rows, lower_end, upper_end, per_group
        )
        attn_probs = jnp.where(
            usable, jnp.exp(head_scores(query_heads, key_block, factor) - log_mass[..., None]), 0.0
        )
        weights = attn_probs.astype(jnp.bfloat16)
        prob_grads = jnp.einsum(
            "qhd,khd->hqk", grad_heads, val_block, preferred_element_type=jnp.float32
        )
        score_grads = (attn_probs * (prob_grads - row_dot[..., None])).astype(jnp.bfloat16)
        query_acc = (
            query_acc
            + jnp.einsum("hqk,khd->qhd", score_grads, key_block, preferred_element_type=jnp.float32)
            * factor
        )
        key_part = (
            jnp.einsum("hqk,qhd->khd", score_grads, query_heads, preferred_element_type=jnp.float32)
            * factor
        )
        val_part = jnp.einsum(
            "hqk,qhd->khd", weights, grad_heads, preferred_element_type=jnp.float32
        )
        key_terms = lax.dynamic_update_slice_in_dim(
            key_terms,
            lax.dynamic_slice_in_dim(key_terms, offset, key_rows, 0) + key_part,
            offset,
            0,
        )
        val_terms = lax.dynamic_update_slice_in_dim(
            val_terms,
            lax.dynamic_slice_in_dim(val_terms, offset, key_rows, 0) + val_part,
            offset,
            0,
        )
        return (query_acc, key_terms, val_terms)

    return lax.fori_loop(begin_block, end_block, summary_advance, carried)


def per_device(queries, key_vectors, value_vectors, out_grads, extra_blocks, summary_rows):
    query_all, key_all, val_all, grad_all = (
        lax.all_to_all(queries, "head", split_axis=1, concat_axis=0, tiled=True),
        lax.all_to_all(key_vectors, "head", split_axis=1, concat_axis=0, tiled=True),
        lax.all_to_all(value_vectors, "head", split_axis=1, concat_axis=0, tiled=True),
        lax.all_to_all(out_grads, "head", split_axis=1, concat_axis=0, tiled=True),
    )
    group_len, local_width = query_all.shape
    head_count = local_width // HD
    factor = HD ** (-0.5)
    query_heads = query_all.reshape(group_len, head_count, HD)
    key_heads = key_all.reshape(group_len, head_count, HD)
    val_heads = val_all.reshape(group_len, head_count, HD)
    grad_heads = grad_all.reshape(group_len, head_count, HD)
    per_group = summary_rows.shape[1]
    seq_count = lax.axis_size("seq")
    group_id = lax.axis_index("seq")
    picker = summary_rows[0][:, None] == jnp.arange(group_len, dtype=jnp.int32)[None, :]
    own_keys = jnp.dot(
        picker.astype(jnp.bfloat16), key_all, preferred_element_type=jnp.float32
    ).astype(jnp.bfloat16)
    own_vals = jnp.dot(
        picker.astype(jnp.bfloat16), val_all, preferred_element_type=jnp.float32
    ).astype(jnp.bfloat16)
    summ_keys_flat, summ_vals_flat = (
        lax.all_gather(own_keys, "seq", axis=0, tiled=True),
        lax.all_gather(own_vals, "seq", axis=0, tiled=True),
    )
    total_rows = summ_keys_flat.shape[0]
    summary_keys = summ_keys_flat.reshape(total_rows, head_count, HD)
    summary_vals = summ_vals_flat.reshape(total_rows, head_count, HD)
    key_rows = per_group * math.gcd(seq_count, max(1, 128 // per_group))
    allowed = local_allowed(extra_blocks[0], group_len)
    local_scores = jnp.where(allowed[None], head_scores(query_heads, key_heads, factor), neg_big)
    local_peak = jnp.max(local_scores, axis=2)
    local_stats = (local_peak, jnp.sum(jnp.exp(local_scores - local_peak[..., None]), axis=2))
    all_stats = merge_stats(
        local_stats,
        softmax_stats(
            query_heads, summary_keys, summary_vals, 0, group_id, key_rows, per_group, factor
        ),
    )
    log_mass = all_stats[0] + jnp.log(all_stats[1])
    summ_values = weighted_values(
        query_heads, log_mass, summary_keys, summary_vals, 0, group_id, key_rows, per_group, factor
    )
    local_probs = jnp.exp(local_scores - log_mass[..., None])
    local_weights = local_probs.astype(jnp.bfloat16)
    attention = (
        summ_values
        + jnp.einsum("hqk,khd->qhd", local_weights, val_heads, preferred_element_type=jnp.float32)
    ).astype(jnp.bfloat16)
    row_dot = jnp.einsum("qhd,qhd->hq", grad_heads, attention, preferred_element_type=jnp.float32)
    local_prob_grads = jnp.einsum(
        "qhd,khd->hqk", grad_heads, val_heads, preferred_element_type=jnp.float32
    )
    local_score_grads = (local_probs * (local_prob_grads - row_dot[..., None])).astype(jnp.bfloat16)
    query_local = (
        jnp.einsum("hqk,khd->qhd", local_score_grads, key_heads, preferred_element_type=jnp.float32)
        * factor
    )
    key_local = (
        jnp.einsum(
            "hqk,qhd->khd", local_score_grads, query_heads, preferred_element_type=jnp.float32
        )
        * factor
    )
    val_local = jnp.einsum(
        "hqk,qhd->khd", local_weights, grad_heads, preferred_element_type=jnp.float32
    )
    empty_terms = jnp.zeros((total_rows, head_count, HD), jnp.float32)
    start_running = (jnp.zeros(query_heads.shape, jnp.float32), empty_terms, empty_terms)
    query_summ, key_terms, val_terms = summary_backward(
        query_heads,
        grad_heads,
        log_mass,
        row_dot,
        summary_keys,
        summary_vals,
        0,
        group_id,
        key_rows,
        per_group,
        factor,
        start_running,
    )
    recv_keys, recv_vals = (
        lax.all_to_all(
            key_terms.astype(jnp.bfloat16), "seq", split_axis=0, concat_axis=0, tiled=True
        ).astype(key_terms.dtype),
        lax.all_to_all(
            val_terms.astype(jnp.bfloat16), "seq", split_axis=0, concat_axis=0, tiled=True
        ).astype(val_terms.dtype),
    )
    summ_key_grad = jnp.sum(recv_keys.reshape(seq_count, per_group, head_count, HD), axis=0)
    summ_val_grad = jnp.sum(recv_vals.reshape(seq_count, per_group, head_count, HD), axis=0)
    picker_f = picker.astype(jnp.float32)
    key_grad = key_local + jnp.einsum(
        "sq,shd->qhd", picker_f, summ_key_grad, precision=lax.Precision.HIGHEST
    )
    value_grad = val_local + jnp.einsum(
        "sq,shd->qhd", picker_f, summ_val_grad, precision=lax.Precision.HIGHEST
    )
    query_grad = query_local + query_summ
    outputs = (
        attention.reshape(group_len, local_width),
        query_grad.astype(jnp.bfloat16).reshape(group_len, local_width),
        key_grad.astype(jnp.bfloat16).reshape(group_len, local_width),
        value_grad.astype(jnp.bfloat16).reshape(group_len, local_width),
    )
    attention_out, query_out, key_out, value_out = (
        lax.all_to_all(outputs[0], "head", split_axis=0, concat_axis=1, tiled=True),
        lax.all_to_all(outputs[1], "head", split_axis=0, concat_axis=1, tiled=True),
        lax.all_to_all(outputs[2], "head", split_axis=0, concat_axis=1, tiled=True),
        lax.all_to_all(outputs[3], "head", split_axis=0, concat_axis=1, tiled=True),
    )
    return (attention_out, query_out, key_out, value_out)


def solution(mesh):
    placed = (
        P(("seq", "head"), None),
        P(("seq", "head"), None),
        P(("seq", "head"), None),
        P(("seq", "head"), None),
        P("seq", None, None),
        P("seq", None),
    )
    return jax.shard_map(
        per_device,
        mesh=mesh,
        in_specs=placed,
        out_specs=(
            P(("seq", "head"), None),
            P(("seq", "head"), None),
            P(("seq", "head"), None),
            P(("seq", "head"), None),
        ),
        check_vma=False,
    )
```

profile of v0, /device:TPU:6, one launch (start us, length us, event | category | flops | bytes accessed | tf_op | source)
XLA Modules:
  0.0 466.3 jit_solution(16607024284181382886)
XLA Ops:
  7.2 2.0 copy.238
  9.2 7.2 %all-to-all-start.2 = ((bf16[64,8,512]{2,0,1:T(8,128)(2,1)}), bf16[64,8,512]{2,0,1:T(8,128)(2,1)S(1)}, u32[]{:S(2)}, u32[]{:S(2)}) async-start(bf16[64,8,512]{2,0,1:T(8,128)(2,1)} %bitcast.103), calls=%async_computation.2 | async-start | bytes 1048576 | tf_op jit(solution)/shard_map/all_to_all | solution.py:163
  16.4 1.9 copy.239
  18.3 15.6 %all-to-all-done.2 = bf16[64,8,512]{2,0,1:T(8,128)(2,1)S(1)} async-done(((bf16[64,8,512]{2,0,1:T(8,128)(2,1)}), bf16[64,8,512]{2,0,1:T(8,128)(2,1)S(1)}, u32[]{:S(2)}, u32[]{:S(2)}) %all-to-all-start.2) | async-done | bytes 524320 | tf_op jit(solution)/shard_map/all_to_all | solution.py:163
  33.9 3.5 all-to-all-start.1
  38.2 17.0 %all-to-all-done.1 = bf16[64,8,512]{2,0,1:T(8,128)(2,1)S(1)} async-done(((bf16[64,8,512]{2,0,1:T(8,128)(2,1)}), bf16[64,8,512]{2,0,1:T(8,128)(2,1)S(1)}, u32[]{:S(2)}, u32[]{:S(2)}) %all-to-all-start.1) | async-done | bytes 524320 | tf_op jit(solution)/shard_map/all_to_all | solution.py:164
  55.3 3.5 all-to-all-start
  60.5 16.1 %all-to-all-done = bf16[64,8,512]{2,0,1:T(8,128)(2,1)S(1)} async-done(((bf16[64,8,512]{2,0,1:T(8,128)(2,1)}), bf16[64,8,512]{2,0,1:T(8,128)(2,1)S(1)}, u32[]{:S(2)}, u32[]{:S(2)}) %all-to-all-start) | async-done | bytes 524320 | tf_op jit(solution)/shard_map/all_to_all | solution.py:165
  76.6 3.5 all-to-all-start.4
  82.6 15.4 %all-to-all-done.4 = bf16[64,8,512]{2,0,1:T(8,128)(2,1)S(1)} async-done(((bf16[64,8,512]{2,0,1:T(8,128)(2,1)}), bf16[64,8,512]{2,0,1:T(8,128)(2,1)S(1)}, u32[]{:S(2)}, u32[]{:S(2)}) %all-to-all-start.4) | async-done | bytes 524320 | tf_op jit(solution)/shard_map/all_to_all | solution.py:166
  99.1 2.0 fusion.37
  101.1 1.9 copy-done.4
  104.0 45.3 %all-gather.5.cloned.1.call-done = bf16[1024,512]{1,0:T(8,128)(2,1)} async-done(((bf16[16,512]{1,0:T(8,128)(2,1)}), bf16[1024,512]{1,0:T(8,128)(2,1)}) %all-gather.5.cloned.1.call-update) | async-done | bytes 1048592 | tf_op jit(solution)/shard_map/all_gather | solution.py:186
  149.3 1.4 copy_bitcast_fusion
  150.7 3.5 while.42
  154.2 78.8 %all-gather.3.cloned.1.call-done = bf16[1024,512]{1,0:T(8,128)(2,1)} async-done(((bf16[16,512]{1,0:T(8,128)(2,1)}), bf16[1024,512]{1,0:T(8,128)(2,1)}) %all-gather.3.cloned.1.call-update) | async-done | bytes 1048592 | tf_op jit(solution)/shard_map/all_gather | solution.py:187
  233.0 2.2 reshape.173
  235.3 9.7 %while.43 = (s32[]{:T(128)}, f32[512,4,128]{0,2,1:T(8,128)S(1)}, s32[]{:T(128)}, bf16[1024,4,128]{2,1,0:T(4,128)(2,1)}, s32[]{:T(128)}, /*index=5*/bf16[1024,4,1...) while((s32[]{:T(128)}, f32[512,4,128]{0,2,1:T(8,128)S(1)}, ...), condition=%wide.region_7.8_spmd, body=%wide.region_6.7_spmd.sunk | while | flops 135530880 | bytes 3154739 | solution.py:98
  245.0 1.3 copy.140
  246.3 4.1 bitcast_convert_fusion
  252.8 6.7 %all-to-all-start.3 = ((bf16[8,64,512]{2,1,0:T(8,128)(2,1)}), bf16[8,64,512]{2,1,0:T(8,128)(2,1)}, u32[]{:S(2)}, u32[]{:S(2)}) async-start(bf16[8,64,512]{2,1,0:T(8,128)(2,1)} %all_to_all.125), calls=%async_computation.3 | async-start | bytes 1048576 | tf_op jit(solution)/shard_map/all_to_all | solution.py:272
  259.7 1.7 broadcast_in_dim.98.clone2
  261.4 1.7 broadcast_in_dim.98.clone
  263.0 34.5 %while.44 = (s32[]{:T(128)}, f32[512,4,128]{0,2,1:T(8,128)S(1)}, f32[1024,4,128]{2,1,0:T(4,128)}, f32[1024,4,128]{2,1,0:T(4,128)}, s32[]{:T(128)}, /*index=5*/bf...) while((s32[]{:T(128)}, f32[512,4,128]{0,2,1:T(8,128)S(1)}, ...), condition=%wide.region_9.10_spmd, body=%wide.region_8.9_spmd.sunk | while | flops 338102656 | bytes 12731235 | solution.py:158
  267.6 1.2 copy_dynamic-update-slice_fusion.3
  273.4 1.2 copy_dynamic-update-slice_fusion.3
  279.2 1.2 copy_dynamic-update-slice_fusion.3
  284.9 1.1 copy_dynamic-update-slice_fusion.3
  290.6 1.2 copy_dynamic-update-slice_fusion.3
  296.4 1.2 copy_dynamic-update-slice_fusion.3
  297.9 4.0 multiply_convert_fusion
  304.7 7.2 %all-to-all-start.5 = ((bf16[8,64,512]{2,1,0:T(8,128)(2,1)}), bf16[8,64,512]{2,1,0:T(8,128)(2,1)S(1)}, u32[]{:S(2)}, u32[]{:S(2)}) async-start(bf16[8,64,512]{2,1,0:T(8,128)(2,1)} %all_to_all.132), calls=%async_computation.5 | async-start | bytes 1048576 | tf_op jit(solution)/shard_map/all_to_all | solution.py:273
  311.9 2.9 convert_element_type.57
  314.8 10.5 %all-to-all-done.5 = bf16[8,64,512]{2,1,0:T(8,128)(2,1)S(1)} async-done(((bf16[8,64,512]{2,1,0:T(8,128)(2,1)}), bf16[8,64,512]{2,1,0:T(8,128)(2,1)S(1)}, u32[]{:S(2)}, u32[]{:S(2)}) %all-to-all-start.5) | async-done | bytes 524320 | tf_op jit(solution)/shard_map/all_to_all | solution.py:273
  326.1 26.3 %all-to-all-start.6 = ((bf16[1024,4,128]{2,1,0:T(4,128)(2,1)}), bf16[1024,4,128]{2,1,0:T(4,128)(2,1)S(1)}, u32[]{:S(2)}, u32[]{:S(2)}) async-start(bf16[1024,4,128]{2,1,0:T(4,128)(2,1)} %convert_element_type.57), calls=%async_computation.6 | async-start | bytes 2097152 | tf_op jit(solution)/shard_map/all_to_all | solution.py:248
  352.4 1.3 convert_element_type.59
  353.7 25.3 %all-to-all-done.6 = bf16[1024,4,128]{2,1,0:T(4,128)(2,1)S(1)} async-done(((bf16[1024,4,128]{2,1,0:T(4,128)(2,1)}), bf16[1024,4,128]{2,1,0:T(4,128)(2,1)S(1)}, u32[]{:S(2)}, u32[]{:S(2)}) %all-to-all-start.6) | async-done | bytes 1048608 | tf_op jit(solution)/shard_map/all_to_all | solution.py:248
  379.0 1.1 copy-done.5
  380.1 8.1 %all-to-all-start.8 = ((bf16[1024,4,128]{2,1,0:T(4,128)(2,1)}), bf16[1024,4,128]{2,1,0:T(4,128)(2,1)S(1)}, u32[]{:S(2)}, u32[]{:S(2)}) async-start(bf16[1024,4,128]{2,1,0:T(4,128)(2,1)} %convert_element_type.59), calls=%async_computation.8 | async-start | bytes 2097152 | tf_op jit(solution)/shard_map/all_to_all | solution.py:251
  388.2 2.5 fusion.39
  393.3 21.5 %all-to-all-done.8 = bf16[1024,4,128]{2,1,0:T(4,128)(2,1)S(1)} async-done(((bf16[1024,4,128]{2,1,0:T(4,128)(2,1)}), bf16[1024,4,128]{2,1,0:T(4,128)(2,1)S(1)}, u32[]{:S(2)}, u32[]{:S(2)}) %all-to-all-start.8) | async-done | bytes 1048608 | tf_op jit(solution)/shard_map/all_to_all | solution.py:251
  414.9 3.5 all-to-all-start.7
  418.4 3.3 convolution_bitcast_fusion.2
  423.2 1.0 all_to_all.142
  424.3 12.8 %all-to-all-done.7 = bf16[8,64,512]{2,1,0:T(8,128)(2,1)S(1)} async-done(((bf16[8,64,512]{2,1,0:T(8,128)(2,1)}), bf16[8,64,512]{2,1,0:T(8,128)(2,1)S(1)}, u32[]{:S(2)}, u32[]{:S(2)}) %all-to-all-start.7) | async-done | bytes 524320 | tf_op jit(solution)/shard_map/all_to_all | solution.py:274
  437.1 3.5 all-to-all-start.9
  440.6 1.9 copy.193
  444.2 14.4 %all-to-all-done.9 = bf16[8,64,512]{2,1,0:T(8,128)(2,1)S(1)} async-done(((bf16[8,64,512]{2,1,0:T(8,128)(2,1)}), bf16[8,64,512]{2,1,0:T(8,128)(2,1)S(1)}, u32[]{:S(2)}, u32[]{:S(2)}) %all-to-all-start.9) | async-done | bytes 524320 | tf_op jit(solution)/shard_map/all_to_all | solution.py:275
  (182 shorter events, 60.1 us)
Async XLA Ops:
  7.2 30.2 %copy-start.12 = (bf16[64,4096]{1,0:T(8,128)(2,1)S(1)}, bf16[64,4096]{1,0:T(8,128)(2,1)}, u32[]{:S(2)}) copy-start(bf16[64,4096]{1,0:T(8,128)(2,1)} %param.14) | copy-start | bytes 1572868
  7.2 51.6 %copy-start.14 = (s32[1,16]{1,0:T(1,128)S(1)}, s32[1,16]{1,0:T(1,128)}, u32[]{:S(2)}) copy-start(s32[1,16]{1,0:T(1,128)} %param.17) | copy-start | bytes 196
  7.2 52.5 %copy-start.13 = (bf16[64,4096]{1,0:T(8,128)(2,1)S(1)}, bf16[64,4096]{1,0:T(8,128)(2,1)}, u32[]{:S(2)}) copy-start(bf16[64,4096]{1,0:T(8,128)(2,1)} %param.15) | copy-start | bytes 1572868
  9.2 71.0 %copy-start.15 = (s32[1,8,8]{2,1,0:T(8,128)S(1)}, s32[1,8,8]{2,1,0:T(8,128)}, u32[]{:S(2)}) copy-start(s32[1,8,8]{2,1,0:T(8,128)} %param.16) | copy-start | bytes 772
  9.2 24.7 %all-to-all-start.2 = ((bf16[64,8,512]{2,0,1:T(8,128)(2,1)}), bf16[64,8,512]{2,0,1:T(8,128)(2,1)S(1)}, u32[]{:S(2)}, u32[]{:S(2)}) async-start(bf16[64,8,512]{2,0,1:T(8,128)(2,1)} %bitcast.103), calls=%async_computation.2 | async-start | bytes 1048576 | tf_op jit(solution)/shard_map/all_to_all | solution.py:163
  33.9 21.4 %all-to-all-start.1 = ((bf16[64,8,512]{2,0,1:T(8,128)(2,1)}), bf16[64,8,512]{2,0,1:T(8,128)(2,1)S(1)}, u32[]{:S(2)}, u32[]{:S(2)}) async-start(bf16[64,8,512]{2,0,1:T(8,128)(2,1)} %bitcast.104), calls=%async_computation.1 | async-start | bytes 1048576 | tf_op jit(solution)/shard_map/all_to_all | solution.py:164
  55.3 21.4 %all-to-all-start = ((bf16[64,8,512]{2,0,1:T(8,128)(2,1)}), bf16[64,8,512]{2,0,1:T(8,128)(2,1)S(1)}, u32[]{:S(2)}, u32[]{:S(2)}) async-start(bf16[64,8,512]{2,0,1:T(8,128)(2,1)} %bitcast.105), calls=%async_computation | async-start | bytes 1048576 | tf_op jit(solution)/shard_map/all_to_all | solution.py:165
  58.8 90.5 %all-gather.5.cloned.1.call-start = ((), (), s32[]{:S(2)}) async-start(), calls=%async_computation.11 | async-start | bytes 1064960 | tf_op jit(solution)/shard_map/all_gather | solution.py:186
  76.6 21.4 %all-to-all-start.4 = ((bf16[64,8,512]{2,0,1:T(8,128)(2,1)}), bf16[64,8,512]{2,0,1:T(8,128)(2,1)S(1)}, u32[]{:S(2)}, u32[]{:S(2)}) async-start(bf16[64,8,512]{2,0,1:T(8,128)(2,1)} %bitcast.102), calls=%async_computation.4 | async-start | bytes 1048576 | tf_op jit(solution)/shard_map/all_to_all | solution.py:166
  80.1 152.8 %all-gather.3.cloned.1.call-start = ((), (), s32[]{:S(2)}) async-start(), calls=%async_computation.10 | async-start | bytes 1064960 | tf_op jit(solution)/shard_map/all_gather | solution.py:187
  80.7 20.4 %copy-start.8 = (bf16[512,4,128]{2,1,0:T(4,128)(2,1)}, bf16[512,4,128]{2,1,0:T(4,128)(2,1)S(1)}, u32[]{:S(2)}) copy-start(bf16[512,4,128]{2,1,0:T(4,128)(2,1)S(1)} %reshape.175) | copy-start | bytes 1572868
  98.1 5.8 %copy-start.1 = (bf16[512,4,128]{2,1,0:T(4,128)(2,1)}, bf16[512,4,128]{2,1,0:T(4,128)(2,1)S(1)}, u32[]{:S(2)}) copy-start(bf16[512,4,128]{2,1,0:T(4,128)(2,1)S(1)} %reshape.180) | copy-start | bytes 1572868
  101.1 1.9 copy-start.4
  246.3 4.1 copy-start.2
  252.8 51.8 %all-to-all-start.3 = ((bf16[8,64,512]{2,1,0:T(8,128)(2,1)}), bf16[8,64,512]{2,1,0:T(8,128)(2,1)}, u32[]{:S(2)}, u32[]{:S(2)}) async-start(bf16[8,64,512]{2,1,0:T(8,128)(2,1)} %all_to_all.125), calls=%async_computation.3 | async-start | bytes 1048576 | tf_op jit(solution)/shard_map/all_to_all | solution.py:272
  297.9 4.0 copy-start.11
  301.9 1.4 copy-start.7
  303.3 49.1 %copy-start = (f32[1024,4,128]{2,1,0:T(4,128)S(1)}, f32[1024,4,128]{2,1,0:T(4,128)}, u32[]{:S(2)}) copy-start(f32[1024,4,128]{2,1,0:T(4,128)} %get-tuple-element.363) | copy-start | bytes 6291460
  304.7 20.6 %all-to-all-start.5 = ((bf16[8,64,512]{2,1,0:T(8,128)(2,1)}), bf16[8,64,512]{2,1,0:T(8,128)(2,1)S(1)}, u32[]{:S(2)}, u32[]{:S(2)}) async-start(bf16[8,64,512]{2,1,0:T(8,128)(2,1)} %all_to_all.132), calls=%async_computation.5 | async-start | bytes 1048576 | tf_op jit(solution)/shard_map/all_to_all | solution.py:273
  325.3 0.8 copy-start.9
  326.1 53.0 %all-to-all-start.6 = ((bf16[1024,4,128]{2,1,0:T(4,128)(2,1)}), bf16[1024,4,128]{2,1,0:T(4,128)(2,1)S(1)}, u32[]{:S(2)}, u32[]{:S(2)}) async-start(bf16[1024,4,128]{2,1,0:T(4,128)(2,1)} %convert_element_type.57), calls=%async_computation.6 | async-start | bytes 2097152 | tf_op jit(solution)/shard_map/all_to_all | solution.py:248
  379.0 1.1 copy-start.5
  380.1 34.8 %all-to-all-start.8 = ((bf16[1024,4,128]{2,1,0:T(4,128)(2,1)}), bf16[1024,4,128]{2,1,0:T(4,128)(2,1)S(1)}, u32[]{:S(2)}, u32[]{:S(2)}) async-start(bf16[1024,4,128]{2,1,0:T(4,128)(2,1)} %convert_element_type.59), calls=%async_computation.8 | async-start | bytes 2097152 | tf_op jit(solution)/shard_map/all_to_all | solution.py:251
  388.2 2.5 copy-start.6
  388.2 30.1 %copy-start.3 = (bf16[512,4,128]{2,1,0:T(4,128)(2,1)S(1)}, bf16[512,4,128]{2,1,0:T(4,128)(2,1)}, u32[]{:S(2)}) copy-start(bf16[512,4,128]{2,1,0:T(4,128)(2,1)} %copy-done.1) | copy-start | bytes 1572868
  414.9 22.2 %all-to-all-start.7 = ((bf16[8,64,512]{2,1,0:T(8,128)(2,1)}), bf16[8,64,512]{2,1,0:T(8,128)(2,1)S(1)}, u32[]{:S(2)}, u32[]{:S(2)}) async-start(bf16[8,64,512]{2,1,0:T(8,128)(2,1)} %all_to_all.137), calls=%async_computation.7 | async-start | bytes 1048576 | tf_op jit(solution)/shard_map/all_to_all | solution.py:274
  421.7 20.8 %copy-start.10 = (bf16[8,64,512]{2,1,0:T(8,128)(2,1)S(1)}, bf16[8,64,512]{2,1,0:T(8,128)(2,1)}, u32[]{:S(2)}) copy-start(bf16[8,64,512]{2,1,0:T(8,128)(2,1)} %copy-done.9) | copy-start | bytes 1572868
  437.1 21.5 %all-to-all-start.9 = ((bf16[8,64,512]{2,1,0:T(8,128)(2,1)}), bf16[8,64,512]{2,1,0:T(8,128)(2,1)S(1)}, u32[]{:S(2)}, u32[]{:S(2)}) async-start(bf16[8,64,512]{2,1,0:T(8,128)(2,1)} %all_to_all.142), calls=%async_computation.9 | async-start | bytes 1048576 | tf_op jit(solution)/shard_map/all_to_all | solution.py:275
Sparse Core Ops, SparseCore 0:
  63.0 86.2 all-gather.4
  153.2 79.7 all-gather.2
where the time goes:
time: 470 us; the launch traced here: 466 us
  waiting for transfers between devices  273 us (58%)
  starting transfers between devices  73.1 us (16%)
  local copies, waits for them, and re-layouts  61.3 us (13%)
  matrix products  35.3 us (8%)
  between operations  14.5 us (3%)
  other arithmetic  8.43 us (2%)
    all_gather x1, waiting for transfers between devices, per_device(): lax.all_gather(own_vals, 'seq', axis=0, tiled=True)  78.8 us
    all_gather x1, waiting for transfers between devices, per_device(): lax.all_gather(own_keys, 'seq', axis=0, tiled=True)  45.3 us
    all_to_all x1, starting transfers between devices, per_device(): lax.all_to_all(key_terms.astype(jnp.bfloat16), 'seq', split_axis=0, conca...  26.3 us
    all_to_all x1, waiting for transfers between devices, per_device(): lax.all_to_all(key_terms.astype(jnp.bfloat16), 'seq', split_axis=0, conca...  25.3 us
    all_to_all x1, waiting for transfers between devices, per_device(): lax.all_to_all(val_terms.astype(jnp.bfloat16), 'seq', split_axis=0, conca...  21.5 us
    all_to_all x1, waiting for transfers between devices, per_device(): lax.all_to_all(key_vectors, 'head', split_axis=1, concat_axis=0, tiled=True)  17 us
    all_to_all x1, waiting for transfers between devices, per_device(): lax.all_to_all(value_vectors, 'head', split_axis=1, concat_axis=0, tiled=...  16.1 us
    all_to_all x1, waiting for transfers between devices, per_device(): lax.all_to_all(queries, 'head', split_axis=1, concat_axis=0, tiled=True)  15.6 us
  transfers between devices with their start and end apart: 12, of which 11 were waited for; matrix products, arithmetic and copies ran while one was open for 16% of the time, Pallas kernels for 0%

commit v1 on v0

v1 whole, which is shorter than its diff:
```python
import functools
import math

import jax
import jax.numpy as jnp
from jax import lax
from jax.experimental import pallas as pl
from jax.experimental.pallas import tpu as pltpu
from jax.sharding import PartitionSpec as P

HD = 128
BF = jnp.bfloat16
F32 = jnp.float32
BIG = 3.0e38
NEG = -1.0e30


def split_seq(count):
    return {64: (4, 8, 2), 8: (2, 2, 2)}[count]


def dot_nn(a, b):
    return lax.dot_general(a, b, (((1,), (0,)), ((), ())), preferred_element_type=F32)


def dot_nt(a, b):
    return lax.dot_general(a, b, (((1,), (1,)), ((), ())), preferred_element_type=F32)


def dot_tn(a, b):
    return lax.dot_general(a, b, (((0,), (0,)), ((), ())), preferred_element_type=F32)


def spread(n):
    order = []
    for d in range(1, n // 2 + 1):
        order.append(d)
        if n - d != d:
            order.append(n - d)
    return order


def kernel(
    cfg,
    q_in, k_in, v_in, g_in, rows_ref, extra_ref,
    o_out, dq_out, dk_out, dv_out,
    kv, qg, skv, cap, sbuf, ebuf, stage, dloc, part, red1, red2, red3, psum,
    in_kv_send, in_qg_send, kv_recv, qg_recv,
    zg_send, zg_recv, xg_send, xg_recv, cg_send, cg_recv,
    cs_send, cs_recv, xs_send, xs_recv, zs_send, zs_recv,
    out_send, out_recv,
):
    nx, nz, nc, ny, heads, rows, summ, nblk = cfg
    group = rows * ny
    zrows = nz * summ
    tile = nc * zrows
    ins = (k_in, v_in, q_in, g_in)
    outs = (o_out, dq_out, dk_out, dv_out)
    factor = HD ** (-0.5)
    coef = factor * math.log2(math.e)

    seq = lax.axis_index("seq")
    y = lax.axis_index("head")
    x = seq // (nz * nc)
    z = (seq // nc) % nz
    c = seq % nc

    def at_y(yp):
        return (seq, yp)

    def at_z(zp):
        return (x * (nz * nc) + zp * nc + c, y)

    def at_x(xp):
        return (xp * (nz * nc) + z * nc + c, y)

    other = (x * (nz * nc) + z * nc + (1 - c), y)

    def remote(src, dst, send, recv, dev):
        return pltpu.make_async_remote_copy(
            src_ref=src, dst_ref=dst, send_sem=send, recv_sem=recv,
            device_id=dev, device_id_type=pl.DeviceIdType.MESH,
        )

    peers = [at_y(lax.rem(y + d, ny)) for d in range(1, ny)]
    peers += [at_z(lax.rem(z + d, nz)) for d in range(1, nz)]
    peers += [at_x(lax.rem(x + d, nx)) for d in range(1, nx)]
    peers += [other]
    barrier = pltpu.get_barrier_semaphore()
    for dev in peers:
        pl.semaphore_signal(barrier, inc=1, device_id=dev, device_id_type=pl.DeviceIdType.MESH)
    pl.semaphore_wait(barrier, len(peers))

    def cols(owner, h):
        return pl.ds(pl.multiple_of((owner * heads + h) * HD, HD), HD)

    def own_rows(owner):
        return pl.ds(pl.multiple_of(owner * rows, rows), rows)

    def send_inputs(h, buf, pair, send, recv):
        for a in range(2):
            pltpu.make_async_copy(
                ins[pair + a].at[:, cols(y, h)], buf.at[h, a, own_rows(y), :], recv.at[h]
            ).start()
        for d in spread(ny):
            yp = lax.rem(y + d, ny)
            for a in range(2):
                remote(
                    ins[pair + a].at[:, cols(yp, h)], buf.at[h, a, own_rows(y), :],
                    send, recv.at[h], at_y(yp),
                ).start()

    @pl.loop(0, heads)
    def _(h):
        send_inputs(h, kv, 0, in_kv_send, kv_recv)

    @pl.loop(0, heads)
    def _(h):
        send_inputs(h, qg, 2, in_qg_send, qg_recv)

    def drain(ref, sem):
        pltpu.make_async_copy(ref, ref, sem).wait()

    onehot = (
        lax.broadcasted_iota(jnp.int32, (summ, group), 1) == rows_ref[...]
    ).astype(F32).astype(BF)

    blen = group // nblk
    ids = lax.broadcasted_iota(jnp.int32, (nblk, group), 0)
    pos = lax.broadcasted_iota(jnp.int32, (nblk, group), 1)
    block_hot = (pos // blen == ids).astype(F32)
    chosen = (extra_ref[...] == 1).astype(F32)
    by_key = dot_nn(chosen, block_hot)
    reads = dot_tn(by_key, block_hot)
    key_pos = lax.broadcasted_iota(jnp.int32, (group, group), 0)
    query_pos = lax.broadcasted_iota(jnp.int32, (group, group), 1)
    lag = query_pos // blen - key_pos // blen
    allowed = (key_pos <= query_pos) & ((lag == 0) | (lag == 1) | ((lag > 0) & (reads > 0.5)))
    cap[...] = jnp.where(allowed, BIG, NEG)

    zslot = pl.ds(pl.multiple_of(z * summ, summ), summ)

    def gather_z(h):
        drain(kv.at[h], kv_recv.at[h])
        for a in range(2):
            skv[h, a, x, c, zslot, :] = dot_nn(onehot, kv[h, a]).astype(BF)
        for d in spread(nz):
            mine = skv.at[h, :, x, c, zslot, :]
            remote(mine, mine, zg_send, zg_recv.at[h], at_z(lax.rem(z + d, nz))).start()

    def gather_x(h):
        drain(skv.at[h, :, 0, 0, pl.ds(0, (nz - 1) * summ), :], zg_recv.at[h])
        for d in spread(nx):
            mine = skv.at[h, :, x, c]
            remote(mine, mine, xg_send, xg_recv.at[h], at_x(lax.rem(x + d, nx))).start()

    def gather_c(h):
        drain(skv.at[h, :, pl.ds(0, nx - 1), 0], xg_recv.at[h])
        mine = skv.at[h, :, :, c]
        remote(mine, mine, cg_send, cg_recv.at[h], other).start()

    @pl.loop(0, heads + 2)
    def _(t):
        @pl.when(t < heads)
        def _():
            gather_z(t)

        @pl.when((t >= 1) & (t < heads + 1))
        def _():
            gather_x(t - 1)

        @pl.when(t >= 2)
        def _():
            gather_c(t - 2)

    row_id = lax.broadcasted_iota(jnp.int32, (tile, 1), 0)
    row_order = ((row_id % zrows) // summ) * nc + row_id // zrows
    is_before = row_order < z * nc + c

    def send_outputs(h, arrays):
        for a in arrays:
            pltpu.make_async_copy(
                stage.at[h, a, own_rows(y), :], outs[a].at[:, cols(y, h)], out_recv.at[a]
            ).start()
        for d in spread(ny):
            yp = lax.rem(y + d, ny)
            for a in arrays:
                remote(
                    stage.at[h, a, own_rows(yp), :], outs[a].at[:, cols(y, h)],
                    out_send, out_recv.at[a], at_y(yp),
                ).start()

    def tile_rows(xp):
        return pl.ds(pl.multiple_of(group + xp * tile, tile), tile)

    def summary_tile(h, a, xp):
        return skv[h, a, xp].reshape(tile, HD)

    def attend(h):
        drain(qg.at[h], qg_recv.at[h])
        drain(skv.at[h, :, :, 0], cg_recv.at[h])
        q = qg[h, 0]
        scores = jnp.minimum(dot_nt(kv[h, 0], q), cap[...])
        sbuf[pl.ds(0, group), :] = scores
        peak = jnp.max(scores, axis=0, keepdims=True)

        def score_tile(xp, peak):
            scores = dot_nt(summary_tile(h, 0, xp), q)
            scores = jnp.minimum(scores, jnp.where((xp < x) | is_before, BIG, NEG))
            sbuf[tile_rows(xp), :] = scores
            return jnp.maximum(peak, jnp.max(scores, axis=0, keepdims=True))

        peak = lax.fori_loop(0, x + 1, score_tile, peak) * coef

        def exp_rows(place, vals, carried):
            mass, acc = carried
            e = jnp.exp2(sbuf[place, :] * coef - peak)
            eb = e.astype(BF)
            ebuf[place, :] = eb
            return mass + jnp.sum(e, axis=0, keepdims=True), acc + dot_tn(vals, eb)

        carried = (jnp.zeros((1, group), F32), jnp.zeros((HD, group), F32))
        carried = exp_rows(pl.ds(0, group), kv[h, 1], carried)
        mass, acc = lax.fori_loop(
            0, x + 1, lambda xp, cr: exp_rows(tile_rows(xp), summary_tile(h, 1, xp), cr), carried
        )
        inv = 1.0 / mass
        attn = (acc * inv).astype(BF).astype(F32)
        stage[h, 0] = attn.T.astype(BF)
        grad_t = qg[h, 1].astype(F32).T
        dot_row = jnp.sum(grad_t * attn, axis=0, keepdims=True) * inv
        grad_ts = grad_t * inv
        grad_tb = grad_ts.astype(BF)
        grad_b = grad_ts.T.astype(BF)

        def back_rows(place, keys, vals, acc):
            eb = ebuf[place, :]
            ds = (eb.astype(F32) * (dot_nn(vals, grad_tb) - dot_row)).astype(BF)
            return acc + dot_tn(keys, ds), dot_nn(ds, q) * factor, dot_nn(eb, grad_b)

        acc, dk, dv = back_rows(pl.ds(0, group), kv[h, 0], kv[h, 1], jnp.zeros((HD, group), F32))
        dloc[h, 0] = dk
        dloc[h, 1] = dv

        def back_tile(xp, acc):
            acc, dk, dv = back_rows(
                tile_rows(xp), summary_tile(h, 0, xp), summary_tile(h, 1, xp), acc
            )
            for cc in range(nc):
                part[h, xp, cc, 0] = dk[cc * zrows:(cc + 1) * zrows].astype(BF)
                part[h, xp, cc, 1] = dv[cc * zrows:(cc + 1) * zrows].astype(BF)
            return acc

        acc = lax.fori_loop(0, x + 1, back_tile, acc)
        stage[h, 1] = (acc * factor).T.astype(BF)
        send_outputs(h, (0, 1))

        @pl.loop(x + 1, nx)
        def _(xp):
            part[h, xp] = jnp.zeros(part.shape[2:], BF)

        mine = part.at[h, :, 1 - c]
        remote(mine, red1.at[h], cs_send, cs_recv.at[h], other).start()

    def reduce_c(h):
        drain(red1.at[h], cs_recv.at[h])

        @pl.loop(0, nx)
        def _(xp):
            part[h, xp, c] = (part[h, xp, c].astype(F32) + red1[h, xp].astype(F32)).astype(BF)

        for d in spread(nx):
            xp = lax.rem(x + d, nx)
            remote(part.at[h, xp, c], red2.at[h, x], xs_send, xs_recv.at[h], at_x(xp)).start()

    def reduce_x(h):
        drain(red2.at[h, pl.ds(0, nx - 1)], xs_recv.at[h])
        total = part[h, x, c].astype(F32)
        for d in range(1, nx):
            total += red2[h, lax.rem(x + d, nx)].astype(F32)
        psum[h] = total.astype(BF)
        for d in spread(nz):
            zp = lax.rem(z + d, nz)
            there = pl.ds(pl.multiple_of(zp * summ, summ), summ)
            remote(
                psum.at[h, :, there, :], red3.at[h, z], zs_send, zs_recv.at[h], at_z(zp)
            ).start()

    def reduce_z(h):
        drain(red3.at[h, pl.ds(0, nz - 1)], zs_recv.at[h])
        total = psum[h, :, zslot, :].astype(F32)
        for d in range(1, nz):
            total += red3[h, lax.rem(z + d, nz)].astype(F32)
        for a in range(2):
            high = total[a].astype(BF)
            low = (total[a] - high.astype(F32)).astype(BF)
            full = dloc[h, a] + dot_tn(onehot, high) + dot_tn(onehot, low)
            stage[h, 2 + a] = full.astype(BF)
        send_outputs(h, (2, 3))

    @pl.loop(0, heads + 3)
    def _(t):
        @pl.when(t < heads)
        def _():
            attend(t)

        @pl.when((t >= 1) & (t < heads + 1))
        def _():
            reduce_c(t - 1)

        @pl.when((t >= 2) & (t < heads + 2))
        def _():
            reduce_x(t - 2)

        @pl.when(t >= 3)
        def _():
            reduce_z(t - 3)

    for a in range(4):
        drain(outs[a], out_recv.at[a])
    sent = pl.ds(0, (ny - 1) * rows)
    drain(kv.at[:, :, sent, :], in_kv_send)
    drain(qg.at[:, :, sent, :], in_qg_send)
    drain(stage.at[:, :, sent, :], out_send)
    drain(skv.at[:, :, 0, 0, pl.ds(0, (nz - 1) * summ), :], zg_send)
    drain(skv.at[:, :, pl.ds(0, nx - 1), 0], xg_send)
    drain(skv.at[:, :, :, 0], cg_send)
    drain(red1, cs_send)
    drain(red2.at[:, pl.ds(0, nx - 1)], xs_send)
    drain(red3.at[:, pl.ds(0, nz - 1)], zs_send)


def per_device(queries, key_vectors, value_vectors, out_grads, extra_blocks, summary_rows):
    rows, feat = queries.shape
    ny = lax.axis_size("head")
    nx, nz, nc = split_seq(lax.axis_size("seq"))
    heads = feat // HD // ny
    summ = summary_rows.shape[1]
    nblk = extra_blocks.shape[1]
    group = rows * ny
    zrows = nz * summ
    keys = group + nx * nc * zrows
    cfg = (nx, nz, nc, ny, heads, rows, summ, nblk)
    dma = pltpu.SemaphoreType.DMA
    hbm = pl.BlockSpec(memory_space=pl.ANY)
    vmem = pl.BlockSpec(memory_space=pltpu.VMEM)
    return pl.pallas_call(
        functools.partial(kernel, cfg),
        out_shape=[jax.ShapeDtypeStruct((rows, feat), BF)] * 4,
        in_specs=[hbm] * 4 + [vmem] * 2,
        out_specs=[hbm] * 4,
        scratch_shapes=[
            pltpu.VMEM((heads, 2, group, HD), BF),
            pltpu.VMEM((heads, 2, group, HD), BF),
            pltpu.VMEM((heads, 2, nx, nc, zrows, HD), BF),
            pltpu.VMEM((group, group), F32),
            pltpu.VMEM((keys, group), F32),
            pltpu.VMEM((keys, group), BF),
            pltpu.VMEM((heads, 4, group, HD), BF),
            pltpu.VMEM((heads, 2, group, HD), F32),
            pltpu.VMEM((heads, nx, nc, 2, zrows, HD), BF),
            pltpu.VMEM((heads, nx, 2, zrows, HD), BF),
            pltpu.VMEM((heads, nx, 2, zrows, HD), BF),
            pltpu.VMEM((heads, nz, 2, summ, HD), BF),
            pltpu.VMEM((heads, 2, zrows, HD), BF),
            dma(()), dma(()), dma((heads,)), dma((heads,)),
            dma(()), dma((heads,)), dma(()), dma((heads,)), dma(()), dma((heads,)),
            dma(()), dma((heads,)), dma(()), dma((heads,)), dma(()), dma((heads,)),
            dma(()), dma((4,)),
        ],
        compiler_params=pltpu.CompilerParams(
            collective_id=0, has_side_effects=True, vmem_limit_bytes=48 * 1024 * 1024
        ),
    )(
        queries, key_vectors, value_vectors, out_grads,
        summary_rows.reshape(summ, 1), extra_blocks[0],
    )


def solution(mesh):
    tokens = P(("seq", "head"), None)
    return jax.shard_map(
        per_device,
        mesh=mesh,
        in_specs=(tokens,) * 4 + (P("seq", None, None), P("seq", None)),
        out_specs=(tokens,) * 4,
        check_vma=False,
    )
```

time: 470 us -> 116 us (0.25)
  waiting for transfers between devices: 273 us -> 0 us
  Pallas kernels: 0 us -> 106 us
  starting transfers between devices: 73.1 us -> 0 us
  local copies, waits for them, and re-layouts: 61.3 us -> 8.67 us
  matrix products: 35.3 us -> 0 us
  between operations: 14.5 us -> 0.65 us
  other arithmetic: 8.43 us -> 0 us
    all_to_all x10 -> x0, waiting for transfers between devices: 149 us -> none  [the longest x1 25.3 us: per_device(): lax.all_to_all(key_terms.astype(jnp.bfloat16), 'seq', split_axis=0, conca...]
    all_gather x2 -> x0, waiting for transfers between devices: 124 us -> none  [the longest x1 78.8 us: per_device(): lax.all_gather(own_vals, 'seq', axis=0, tiled=True)]
    pallas_call x0 -> x1, Pallas kernels: none -> 106 us  [per_device(): pl.pallas_call(functools.partial(kernel, cfg), out_shape=[jax.ShapeDtypeS...]
    all_to_all x10 -> x0, starting transfers between devices: 73 us -> none  [the longest x1 26.3 us: per_device(): lax.all_to_all(key_terms.astype(jnp.bfloat16), 'seq', split_axis=0, conca...]
    dot_general x52 -> x0, matrix products: 35.3 us -> none  [the longest x13 6.05 us: head_scores(): jnp.einsum('qhd,khd->hqk', query_heads, key_heads, preferred_element_type...]
    dynamic_slice x24 -> x0, local copies, waits for them, and re-layouts: 23.2 us -> none  [the longest x12 11.5 us: key_window(): val_block = lax.dynamic_slice_in_dim(summary_vals, offset, key_rows, 0)]
    all_to_all x12 -> x0, local copies, waits for them, and re-layouts: 13.9 us -> none  [the longest x2 2.87 us: per_device(): lax.all_to_all(outputs[0], 'head', split_axis=0, concat_axis=1, tiled=True)]
    dynamic_update_slice x6 -> x0, local copies, waits for them, and re-layouts: 6.95 us -> none  [summary_advance(): lax.dynamic_update_slice_in_dim(val_terms, lax.dynamic_slice_in_dim(val_t...]
  transfers between devices with their start and end apart: 12 -> 0, of which waited for: 11 -> 0; matrix products, arithmetic and copies ran while one was open for 16% -> 0% of each run, Pallas kernels for 0% -> 0%
where the time goes in v1:
time: 116 us
  Pallas kernels  106 us (91%)
  local copies, waits for them, and re-layouts  8.67 us (7%)
    pallas_call x1, Pallas kernels, per_device(): pl.pallas_call(functools.partial(kernel, cfg), out_shape=[jax.ShapeDtypeS...  106 us
    unnamed x16, local copies, waits for them, and re-layouts  8.59 us

profile of v1, /device:TPU:6, one launch (start us, length us, event | category | flops | bytes accessed | tf_op | source)
XLA Modules:
  0.0 115.7 jit_solution(3689404630821279997)
XLA Ops:
  0.6 0.0 copy-start.5
  0.6 0.6 copy-done.5
  1.3 0.0 copy-start.4
  1.3 0.1 copy.10.rows_ref
  1.4 0.6 copy-done.4
  2.0 0.0 copy-start
  2.0 1.0 copy-done
  3.0 0.0 copy-start.1
  3.0 1.0 copy-done.1
  4.1 0.0 copy-start.2
  4.1 1.0 copy-done.2
  5.1 0.0 copy-start.3
  5.1 1.0 copy-done.3
  6.1 106.4 %shard_map.93 = (bf16[64,4096]{1,0:T(8,128)(2,1)S(1)}, bf16[64,4096]{1,0:T(8,128)(2,1)S(1)}, bf16[64,4096]{1,0:T(8,128)(2,1)S(1)}, bf16[64,4096]{1,0:T(8,128)(2,1)S(1)}) custom-call(bf16[64,4096]{1,0:T(8,128)(2,1)S(1)} %copy-done, bf16[64,4096]{1,0:T(8,128)(2,1)S(1)} %copy-done.1, bf16[64,4096]{1,0:T(8,128)(2,1)S(1)} %copy-done.2, ...), custom_call_target="tpu_custom_call" | custom-call | tf_op jit(solution)/shard_map/pallas_call | solution.py:347
  112.5 0.8 copy.15
  113.3 0.8 copy.16
  114.1 0.8 copy.17
  114.9 0.8 copy.18
Async XLA Ops:
  0.6 0.7 copy-start.5
  1.3 0.7 copy-start.4
  2.0 1.0 copy-start
  3.0 1.0 copy-start.1
  4.1 1.0 copy-start.2
  5.1 1.0 copy-start.3

commit v2 on v1

--- a/solution.py
+++ b/solution.py
@@ -42,13 +42,13 @@
 
 def kernel(
     cfg,
-    q_in, k_in, v_in, g_in, rows_ref, extra_ref,
+    q_in, k_in, v_in, g_in, rows_in, extra_in,
     o_out, dq_out, dk_out, dv_out,
     kv, qg, skv, cap, sbuf, ebuf, stage, dloc, part, red1, red2, red3, psum,
     in_kv_send, in_qg_send, kv_recv, qg_recv,
     zg_send, zg_recv, xg_send, xg_recv, cg_send, cg_recv,
     cs_send, cs_recv, xs_send, xs_recv, zs_send, zs_recv,
-    out_send, out_recv,
+    out_send, out_recv, rows_ref, extra_ref, small_sem,
 ):
     nx, nz, nc, ny, heads, rows, summ, nblk = cfg
     group = rows * ny
@@ -89,6 +89,12 @@
     barrier = pltpu.get_barrier_semaphore()
     for dev in peers:
         pl.semaphore_signal(barrier, inc=1, device_id=dev, device_id_type=pl.DeviceIdType.MESH)
+    small = (
+        pltpu.make_async_copy(rows_in, rows_ref, small_sem.at[0]),
+        pltpu.make_async_copy(extra_in, extra_ref, small_sem.at[1]),
+    )
+    for copy in small:
+        copy.start()
     pl.semaphore_wait(barrier, len(peers))
 
     def cols(owner, h):
@@ -121,15 +127,17 @@
     def drain(ref, sem):
         pltpu.make_async_copy(ref, ref, sem).wait()
 
+    for copy in small:
+        copy.wait()
     onehot = (
-        lax.broadcasted_iota(jnp.int32, (summ, group), 1) == rows_ref[...]
+        lax.broadcasted_iota(jnp.int32, (group, summ), 0) == rows_ref[...]
     ).astype(F32).astype(BF)
 
     blen = group // nblk
     ids = lax.broadcasted_iota(jnp.int32, (nblk, group), 0)
     pos = lax.broadcasted_iota(jnp.int32, (nblk, group), 1)
     block_hot = (pos // blen == ids).astype(F32)
-    chosen = (extra_ref[...] == 1).astype(F32)
+    chosen = (extra_ref[0] == 1).astype(F32)
     by_key = dot_nn(chosen, block_hot)
     reads = dot_tn(by_key, block_hot)
     key_pos = lax.broadcasted_iota(jnp.int32, (group, group), 0)
@@ -143,7 +151,7 @@
     def gather_z(h):
         drain(kv.at[h], kv_recv.at[h])
         for a in range(2):
-            skv[h, a, x, c, zslot, :] = dot_nn(onehot, kv[h, a]).astype(BF)
+            skv[h, a, x, c, zslot, :] = dot_tn(onehot, kv[h, a]).astype(BF)
         for d in spread(nz):
             mine = skv.at[h, :, x, c, zslot, :]
             remote(mine, mine, zg_send, zg_recv.at[h], at_z(lax.rem(z + d, nz))).start()
@@ -294,7 +302,7 @@
         for a in range(2):
             high = total[a].astype(BF)
             low = (total[a] - high.astype(F32)).astype(BF)
-            full = dloc[h, a] + dot_tn(onehot, high) + dot_tn(onehot, low)
+            full = dloc[h, a] + dot_nn(onehot, high) + dot_nn(onehot, low)
             stage[h, 2 + a] = full.astype(BF)
         send_outputs(h, (2, 3))
 
@@ -328,6 +336,25 @@
     drain(red1, cs_send)
     drain(red2.at[:, pl.ds(0, nx - 1)], xs_send)
     drain(red3.at[:, pl.ds(0, nz - 1)], zs_send)
+
+
+def hand_over(a_in, b_in, c_in, d_in, a_out, b_out, c_out, d_out, buf, in_sems, out_sems):
+    pieces = buf.shape[1]
+    width = buf.shape[3]
+    pairs = ((a_in, a_out), (b_in, b_out), (c_in, c_out), (d_in, d_out))
+    loads, saves = [], []
+    for i, (src, dst) in enumerate(pairs):
+        for j in range(pieces):
+            part = pl.ds(j * width, width)
+            loads.append(pltpu.make_async_copy(src.at[:, part], buf.at[i, j], in_sems.at[i, j]))
+            saves.append(pltpu.make_async_copy(buf.at[i, j], dst.at[:, part], out_sems.at[i, j]))
+    for load in loads:
+        load.start()
+    for load, save in zip(loads, saves):
+        load.wait()
+        save.start()
+    for save in saves:
+        save.wait()
 
 
 def per_device(queries, key_vectors, value_vectors, out_grads, extra_blocks, summary_rows):
@@ -343,11 +370,10 @@
     cfg = (nx, nz, nc, ny, heads, rows, summ, nblk)
     dma = pltpu.SemaphoreType.DMA
     hbm = pl.BlockSpec(memory_space=pl.ANY)
-    vmem = pl.BlockSpec(memory_space=pltpu.VMEM)
-    return pl.pallas_call(
+    parts = pl.pallas_call(
         functools.partial(kernel, cfg),
         out_shape=[jax.ShapeDtypeStruct((rows, feat), BF)] * 4,
-        in_specs=[hbm] * 4 + [vmem] * 2,
+        in_specs=[hbm] * 6,
         out_specs=[hbm] * 4,
         scratch_shapes=[
             pltpu.VMEM((heads, 2, group, HD), BF),
@@ -367,14 +393,24 @@
             dma(()), dma((heads,)), dma(()), dma((heads,)), dma(()), dma((heads,)),
             dma(()), dma((heads,)), dma(()), dma((heads,)), dma(()), dma((heads,)),
             dma(()), dma((4,)),
+            pltpu.VMEM((1, summ), jnp.int32), pltpu.VMEM((1, nblk, nblk), jnp.int32), dma((2,)),
         ],
         compiler_params=pltpu.CompilerParams(
-            collective_id=0, has_side_effects=True, vmem_limit_bytes=48 * 1024 * 1024
+            collective_id=0, has_side_effects=True, vmem_limit_bytes=58 * 1024 * 1024
         ),
     )(
         queries, key_vectors, value_vectors, out_grads,
-        summary_rows.reshape(summ, 1), extra_blocks[0],
+        summary_rows, extra_blocks,
     )
+    return pl.pallas_call(
+        hand_over,
+        out_shape=[jax.ShapeDtypeStruct((rows, feat), BF)] * 4,
+        in_specs=[hbm] * 4,
+        out_specs=[hbm] * 4,
+        scratch_shapes=[
+            pltpu.VMEM((4, 2, rows, feat // 2), BF), dma((4, 2)), dma((4, 2)),
+        ],
+    )(*parts)
 
 
 def solution(mesh):

time: 116 us -> 110 us (0.948)
  local copies, waits for them, and re-layouts: 8.67 us -> 0 us
  Pallas kernels: 106 us -> 109 us
    unnamed x16 -> x0, local copies, waits for them, and re-layouts: 8.59 us -> none
    pallas_call x0 -> x1, Pallas kernels: none -> 2.4 us  [per_device(): pl.pallas_call(hand_over, out_shape=[jax.ShapeDtypeStruct((rows, feat), B...]
where the time goes in v2:
time: 110 us
  Pallas kernels  109 us (99%)
    pallas_call x1, Pallas kernels, per_device(): pl.pallas_call(functools.partial(kernel, cfg), out_shape=[jax.ShapeDtypeS...  107 us
    pallas_call x1, Pallas kernels, per_device(): pl.pallas_call(hand_over, out_shape=[jax.ShapeDtypeStruct((rows, feat), B...  2.4 us

profile of v2, /device:TPU:6, one launch (start us, length us, event | category | flops | bytes accessed | tf_op | source)
XLA Modules:
  0.0 109.8 jit_solution(5239821102767671942)
XLA Ops:
  0.6 106.7 %shard_map.93 = (bf16[64,4096]{1,0:T(8,128)(2,1)}, bf16[64,4096]{1,0:T(8,128)(2,1)}, bf16[64,4096]{1,0:T(8,128)(2,1)}, bf16[64,4096]{1,0:T(8,128)(2,1)}) custom-call(bf16[64,4096]{1,0:T(8,128)(2,1)} %q_in.1, bf16[64,4096]{1,0:T(8,128)(2,1)} %k_in.1, bf16[64,4096]{1,0:T(8,128)(2,1)} %v_in.1, bf16[64,4096]{1,0:T(8,128)(2,1)} %g_in.1, s32[1,16]{1,0:T(1,128)} %rows_in.1, ...), custom_call_target="tpu_custom_call" | custom-call | tf_op jit(solution)/shard_map/pallas_call | solution.py:373
  107.4 2.4 %shard_map.94 = (bf16[64,4096]{1,0:T(8,128)(2,1)}, bf16[64,4096]{1,0:T(8,128)(2,1)}, bf16[64,4096]{1,0:T(8,128)(2,1)}, bf16[64,4096]{1,0:T(8,128)(2,1)}) custom-call(bf16[64,4096]{1,0:T(8,128)(2,1)} %get-tuple-element.8.a_in, bf16[64,4096]{1,0:T(8,128)(2,1)} %get-tuple-element.9.b_in, bf16[64,4096]{1,0:T(8,128)(2,1)} %get-tuple-element.10.c_in, ...), custom_call_target="tpu_custom_call" | custom-call | tf_op jit(solution)/shard_map/pallas_call | solution.py:405

commit v3 on v2

--- a/solution.py
+++ b/solution.py
@@ -48,7 +48,7 @@
     in_kv_send, in_qg_send, kv_recv, qg_recv,
     zg_send, zg_recv, xg_send, xg_recv, cg_send, cg_recv,
     cs_send, cs_recv, xs_send, xs_recv, zs_send, zs_recv,
-    out_send, out_recv, rows_ref, extra_ref, small_sem,
+    out_send, out_recv, rows_ref, extra_ref, small_sem, ring_ready, all_ready,
 ):
     nx, nz, nc, ny, heads, rows, summ, nblk = cfg
     group = rows * ny
@@ -82,20 +82,38 @@
             device_id=dev, device_id_type=pl.DeviceIdType.MESH,
         )
 
-    peers = [at_y(lax.rem(y + d, ny)) for d in range(1, ny)]
-    peers += [at_z(lax.rem(z + d, nz)) for d in range(1, nz)]
-    peers += [at_x(lax.rem(x + d, nx)) for d in range(1, nx)]
-    peers += [other]
+    def signal(sem, dev):
+        pl.semaphore_signal(sem, inc=1, device_id=dev, device_id_type=pl.DeviceIdType.MESH)
+
     barrier = pltpu.get_barrier_semaphore()
-    for dev in peers:
-        pl.semaphore_signal(barrier, inc=1, device_id=dev, device_id_type=pl.DeviceIdType.MESH)
+    for d in range(1, ny):
+        yp = lax.rem(y + d, ny)
+
+        @pl.when(yp != 0)
+        def _():
+            signal(barrier, at_y(yp))
+
     small = (
         pltpu.make_async_copy(rows_in, rows_ref, small_sem.at[0]),
         pltpu.make_async_copy(extra_in, extra_ref, small_sem.at[1]),
     )
     for copy in small:
         copy.start()
-    pl.semaphore_wait(barrier, len(peers))
+
+    @pl.when(y != 0)
+    def _():
+        pl.semaphore_wait(barrier, ny - 1)
+        signal(ring_ready, at_y(0))
+
+    rings = [at_z(lax.rem(z + d, nz)) for d in range(1, nz)]
+    rings += [at_x(lax.rem(x + d, nx)) for d in range(1, nx)]
+    rings += [other]
+
+    @pl.when(y == 0)
+    def _():
+        pl.semaphore_wait(ring_ready, ny - 1)
+        for dev in rings:
+            signal(barrier, dev)
 
     def cols(owner, h):
         return pl.ds(pl.multiple_of((owner * heads + h) * HD, HD), HD)
@@ -166,6 +184,16 @@
         drain(skv.at[h, :, pl.ds(0, nx - 1), 0], xg_recv.at[h])
         mine = skv.at[h, :, :, c]
         remote(mine, mine, cg_send, cg_recv.at[h], other).start()
+
+    @pl.when(y == 0)
+    def _():
+        pl.semaphore_wait(barrier, len(rings))
+        for d in range(1, ny):
+            signal(all_ready, at_y(d))
+
+    @pl.when(y != 0)
+    def _():
+        pl.semaphore_wait(all_ready, 1)
 
     @pl.loop(0, heads + 2)
     def _(t):
@@ -394,6 +422,7 @@
             dma(()), dma((heads,)), dma(()), dma((heads,)), dma(()), dma((heads,)),
             dma(()), dma((4,)),
             pltpu.VMEM((1, summ), jnp.int32), pltpu.VMEM((1, nblk, nblk), jnp.int32), dma((2,)),
+            pltpu.SemaphoreType.REGULAR, pltpu.SemaphoreType.REGULAR,
         ],
         compiler_params=pltpu.CompilerParams(
             collective_id=0, has_side_effects=True, vmem_limit_bytes=58 * 1024 * 1024

time: 110 us -> 107 us (0.973)
  Pallas kernels: 109 us -> 107 us
    pallas_call x1, Pallas kernels: 107 us -> 104 us  [per_device(): pl.pallas_call(functools.partial(kernel, cfg), out_shape=[jax.ShapeDtypeS...]
where the time goes in v3:
time: 107 us
  Pallas kernels  107 us (100%)
    pallas_call x1, Pallas kernels, per_device(): pl.pallas_call(functools.partial(kernel, cfg), out_shape=[jax.ShapeDtypeS...  104 us
    pallas_call x1, Pallas kernels, per_device(): pl.pallas_call(hand_over, out_shape=[jax.ShapeDtypeStruct((rows, feat), B...  2.4 us

profile of v3, /device:TPU:6, one launch (start us, length us, event | category | flops | bytes accessed | tf_op | source)
XLA Modules:
  0.0 107.2 jit_solution(7350420691446279271)
XLA Ops:
  0.6 104.1 %shard_map.93 = (bf16[64,4096]{1,0:T(8,128)(2,1)}, bf16[64,4096]{1,0:T(8,128)(2,1)}, bf16[64,4096]{1,0:T(8,128)(2,1)}, bf16[64,4096]{1,0:T(8,128)(2,1)}) custom-call(bf16[64,4096]{1,0:T(8,128)(2,1)} %q_in.1, bf16[64,4096]{1,0:T(8,128)(2,1)} %k_in.1, bf16[64,4096]{1,0:T(8,128)(2,1)} %v_in.1, bf16[64,4096]{1,0:T(8,128)(2,1)} %g_in.1, s32[1,16]{1,0:T(1,128)} %rows_in.1, ...), custom_call_target="tpu_custom_call" | custom-call | tf_op jit(solution)/shard_map/pallas_call | solution.py:401
  104.8 2.4 %shard_map.94 = (bf16[64,4096]{1,0:T(8,128)(2,1)}, bf16[64,4096]{1,0:T(8,128)(2,1)}, bf16[64,4096]{1,0:T(8,128)(2,1)}, bf16[64,4096]{1,0:T(8,128)(2,1)}) custom-call(bf16[64,4096]{1,0:T(8,128)(2,1)} %get-tuple-element.8.a_in, bf16[64,4096]{1,0:T(8,128)(2,1)} %get-tuple-element.9.b_in, bf16[64,4096]{1,0:T(8,128)(2,1)} %get-tuple-element.10.c_in, ...), custom_call_target="tpu_custom_call" | custom-call | tf_op jit(solution)/shard_map/pallas_call | solution.py:434

commit v4 on v3

--- a/solution.py
+++ b/solution.py
@@ -226,40 +226,34 @@
                     out_send, out_recv.at[a], at_y(yp),
                 ).start()
 
-    def tile_rows(xp):
-        return pl.ds(pl.multiple_of(group + xp * tile, tile), tile)
-
-    def summary_tile(h, a, xp):
-        return skv[h, a, xp].reshape(tile, HD)
-
-    def attend(h):
-        drain(qg.at[h], qg_recv.at[h])
-        drain(skv.at[h, :, :, 0], cg_recv.at[h])
+    def attend(h, tiles):
         q = qg[h, 0]
-        scores = jnp.minimum(dot_nt(kv[h, 0], q), cap[...])
-        sbuf[pl.ds(0, group), :] = scores
-        peak = jnp.max(scores, axis=0, keepdims=True)
-
-        def score_tile(xp, peak):
-            scores = dot_nt(summary_tile(h, 0, xp), q)
-            scores = jnp.minimum(scores, jnp.where((xp < x) | is_before, BIG, NEG))
-            sbuf[tile_rows(xp), :] = scores
-            return jnp.maximum(peak, jnp.max(scores, axis=0, keepdims=True))
-
-        peak = lax.fori_loop(0, x + 1, score_tile, peak) * coef
-
-        def exp_rows(place, vals, carried):
-            mass, acc = carried
+        spans = [(pl.ds(0, group), kv[h, 0], kv[h, 1])]
+        for xp in range(tiles):
+            spans.append((
+                pl.ds(group + xp * tile, tile),
+                skv[h, 0, xp].reshape(tile, HD),
+                skv[h, 1, xp].reshape(tile, HD),
+            ))
+        peak = None
+        for i, (place, keys, _) in enumerate(spans):
+            scores = dot_nt(keys, q)
+            if i == 0:
+                scores = jnp.minimum(scores, cap[...])
+            elif i == tiles:
+                scores = jnp.minimum(scores, jnp.where(is_before, BIG, NEG))
+            sbuf[place, :] = scores
+            top = jnp.max(scores, axis=0, keepdims=True)
+            peak = top if peak is None else jnp.maximum(peak, top)
+        peak = peak * coef
+        mass = jnp.zeros((1, group), F32)
+        acc = jnp.zeros((HD, group), F32)
+        for place, _, vals in spans:
             e = jnp.exp2(sbuf[place, :] * coef - peak)
             eb = e.astype(BF)
             ebuf[place, :] = eb
-            return mass + jnp.sum(e, axis=0, keepdims=True), acc + dot_tn(vals, eb)
-
-        carried = (jnp.zeros((1, group), F32), jnp.zeros((HD, group), F32))
-        carried = exp_rows(pl.ds(0, group), kv[h, 1], carried)
-        mass, acc = lax.fori_loop(
-            0, x + 1, lambda xp, cr: exp_rows(tile_rows(xp), summary_tile(h, 1, xp), cr), carried
-        )
+            mass += jnp.sum(e, axis=0, keepdims=True)
+            acc += dot_tn(vals, eb)
         inv = 1.0 / mass
         attn = (acc * inv).astype(BF).astype(F32)
         stage[h, 0] = attn.T.astype(BF)
@@ -268,32 +262,35 @@
         grad_ts = grad_t * inv
         grad_tb = grad_ts.astype(BF)
         grad_b = grad_ts.T.astype(BF)
-
-        def back_rows(place, keys, vals, acc):
+        acc = jnp.zeros((HD, group), F32)
+        for i, (place, keys, vals) in enumerate(spans):
             eb = ebuf[place, :]
             ds = (eb.astype(F32) * (dot_nn(vals, grad_tb) - dot_row)).astype(BF)
-            return acc + dot_tn(keys, ds), dot_nn(ds, q) * factor, dot_nn(eb, grad_b)
-
-        acc, dk, dv = back_rows(pl.ds(0, group), kv[h, 0], kv[h, 1], jnp.zeros((HD, group), F32))
-        dloc[h, 0] = dk
-        dloc[h, 1] = dv
-
-        def back_tile(xp, acc):
-            acc, dk, dv = back_rows(
-                tile_rows(xp), summary_tile(h, 0, xp), summary_tile(h, 1, xp), acc
-            )
-            for cc in range(nc):
-                part[h, xp, cc, 0] = dk[cc * zrows:(cc + 1) * zrows].astype(BF)
-                part[h, xp, cc, 1] = dv[cc * zrows:(cc + 1) * zrows].astype(BF)
-            return acc
-
-        acc = lax.fori_loop(0, x + 1, back_tile, acc)
+            acc += dot_tn(keys, ds)
+            dk = dot_nn(ds, q) * factor
+            dv = dot_nn(eb, grad_b)
+            if i == 0:
+                dloc[h, 0] = dk
+                dloc[h, 1] = dv
+            else:
+                for cc in range(nc):
+                    rows_c = slice(cc * zrows, (cc + 1) * zrows)
+                    part[h, i - 1, cc, 0] = dk[rows_c].astype(BF)
+                    part[h, i - 1, cc, 1] = dv[rows_c].astype(BF)
         stage[h, 1] = (acc * factor).T.astype(BF)
+        for xp in range(tiles, nx):
+            part[h, xp] = jnp.zeros(part.shape[2:], BF)
+
+    def attend_send(h):
+        drain(qg.at[h], qg_recv.at[h])
+        drain(skv.at[h, :, :, 0], cg_recv.at[h])
+        for tiles in range(1, nx + 1):
+
+            @pl.when(x == tiles - 1)
+            def _():
+                attend(h, tiles)
+
         send_outputs(h, (0, 1))
-
-        @pl.loop(x + 1, nx)
-        def _(xp):
-            part[h, xp] = jnp.zeros(part.shape[2:], BF)
 
         mine = part.at[h, :, 1 - c]
         remote(mine, red1.at[h], cs_send, cs_recv.at[h], other).start()
@@ -338,7 +335,7 @@
     def _(t):
         @pl.when(t < heads)
         def _():
-            attend(t)
+            attend_send(t)
 
         @pl.when((t >= 1) & (t < heads + 1))
         def _():

time: 107 us -> 103 us (0.963)
  Pallas kernels: 107 us -> 103 us
    pallas_call x1, Pallas kernels: 104 us -> 100 us  [per_device(): pl.pallas_call(functools.partial(kernel, cfg), out_shape=[jax.ShapeDtypeS...]
where the time goes in v4:
time: 103 us
  Pallas kernels  103 us (100%)
    pallas_call x1, Pallas kernels, per_device(): pl.pallas_call(functools.partial(kernel, cfg), out_shape=[jax.ShapeDtypeS...  100 us
    pallas_call x1, Pallas kernels, per_device(): pl.pallas_call(hand_over, out_shape=[jax.ShapeDtypeStruct((rows, feat), B...  2.4 us

profile of v4, /device:TPU:6, one launch (start us, length us, event | category | flops | bytes accessed | tf_op | source)
XLA Modules:
  0.0 103.3 jit_solution(3913513509965298000)
XLA Ops:
  0.6 100.3 %shard_map.93 = (bf16[64,4096]{1,0:T(8,128)(2,1)}, bf16[64,4096]{1,0:T(8,128)(2,1)}, bf16[64,4096]{1,0:T(8,128)(2,1)}, bf16[64,4096]{1,0:T(8,128)(2,1)}) custom-call(bf16[64,4096]{1,0:T(8,128)(2,1)} %q_in.1, bf16[64,4096]{1,0:T(8,128)(2,1)} %k_in.1, bf16[64,4096]{1,0:T(8,128)(2,1)} %v_in.1, bf16[64,4096]{1,0:T(8,128)(2,1)} %g_in.1, s32[1,16]{1,0:T(1,128)} %rows_in.1, ...), custom_call_target="tpu_custom_call" | custom-call | tf_op jit(solution)/shard_map/pallas_call | solution.py:398
  100.9 2.4 %shard_map.94 = (bf16[64,4096]{1,0:T(8,128)(2,1)}, bf16[64,4096]{1,0:T(8,128)(2,1)}, bf16[64,4096]{1,0:T(8,128)(2,1)}, bf16[64,4096]{1,0:T(8,128)(2,1)}) custom-call(bf16[64,4096]{1,0:T(8,128)(2,1)} %get-tuple-element.8.a_in, bf16[64,4096]{1,0:T(8,128)(2,1)} %get-tuple-element.9.b_in, bf16[64,4096]{1,0:T(8,128)(2,1)} %get-tuple-element.10.c_in, ...), custom_call_target="tpu_custom_call" | custom-call | tf_op jit(solution)/shard_map/pallas_call | solution.py:431

commit v5 on v4

--- a/solution.py
+++ b/solution.py
@@ -195,13 +195,11 @@
     def _():
         pl.semaphore_wait(all_ready, 1)
 
-    @pl.loop(0, heads + 2)
+    @pl.loop(0, heads)
     def _(t):
-        @pl.when(t < heads)
-        def _():
-            gather_z(t)
-
-        @pl.when((t >= 1) & (t < heads + 1))
+        gather_z(t)
+
+        @pl.when(t >= 1)
         def _():
             gather_x(t - 1)
 
@@ -337,6 +335,15 @@
         def _():
             attend_send(t)
 
+        @pl.when(t == 0)
+        def _():
+            gather_x(heads - 1)
+            gather_c(heads - 2)
+
+        @pl.when(t == 1)
+        def _():
+            gather_c(heads - 1)
+
         @pl.when((t >= 1) & (t < heads + 1))
         def _():
             reduce_c(t - 1)
@@ -363,20 +370,16 @@
     drain(red3.at[:, pl.ds(0, nz - 1)], zs_send)
 
 
-def hand_over(a_in, b_in, c_in, d_in, a_out, b_out, c_out, d_out, buf, in_sems, out_sems):
-    pieces = buf.shape[1]
-    width = buf.shape[3]
+def hand_over(a_in, b_in, c_in, d_in, a_out, b_out, c_out, d_out, sems):
+    pieces = sems.shape[1]
+    width = a_in.shape[1] // pieces
     pairs = ((a_in, a_out), (b_in, b_out), (c_in, c_out), (d_in, d_out))
-    loads, saves = [], []
-    for i, (src, dst) in enumerate(pairs):
-        for j in range(pieces):
+    saves = []
+    for j in range(pieces):
+        for i, (src, dst) in enumerate(pairs):
             part = pl.ds(j * width, width)
-            loads.append(pltpu.make_async_copy(src.at[:, part], buf.at[i, j], in_sems.at[i, j]))
-            saves.append(pltpu.make_async_copy(buf.at[i, j], dst.at[:, part], out_sems.at[i, j]))
-    for load in loads:
-        load.start()
-    for load, save in zip(loads, saves):
-        load.wait()
+            saves.append(pltpu.make_async_copy(src.at[:, part], dst.at[:, part], sems.at[i, j]))
+    for save in saves:
         save.start()
     for save in saves:
         save.wait()
@@ -422,20 +425,23 @@
             pltpu.SemaphoreType.REGULAR, pltpu.SemaphoreType.REGULAR,
         ],
         compiler_params=pltpu.CompilerParams(
-            collective_id=0, has_side_effects=True, vmem_limit_bytes=58 * 1024 * 1024
+            collective_id=0, has_side_effects=True, vmem_limit_bytes=28 * 1024 * 1024
         ),
     )(
-        queries, key_vectors, value_vectors, out_grads,
-        summary_rows, extra_blocks,
+        *(
+            pltpu.with_memory_space_constraint(arg, pltpu.HBM)
+            for arg in (
+                queries, key_vectors, value_vectors, out_grads, summary_rows, extra_blocks
+            )
+        ),
     )
     return pl.pallas_call(
         hand_over,
         out_shape=[jax.ShapeDtypeStruct((rows, feat), BF)] * 4,
         in_specs=[hbm] * 4,
         out_specs=[hbm] * 4,
-        scratch_shapes=[
-            pltpu.VMEM((4, 2, rows, feat // 2), BF), dma((4, 2)), dma((4, 2)),
-        ],
+        scratch_shapes=[dma((4, 2))],
+        compiler_params=pltpu.CompilerParams(vmem_limit_bytes=4 * 1024 * 1024),
     )(*parts)
 
 

time: 103 us -> 100 us (0.971)
  Pallas kernels: 103 us -> 99 us
    pallas_call x1, Pallas kernels: 100 us -> 97.6 us  [per_device(): pl.pallas_call(functools.partial(kernel, cfg), out_shape=[jax.ShapeDtypeS...]
where the time goes in v5:
time: 100 us; the launch traced here: 99.6 us
  Pallas kernels  99 us (99%)
    pallas_call x1, Pallas kernels, per_device(): pl.pallas_call(functools.partial(kernel, cfg), out_shape=[jax.ShapeDtypeS...  97.6 us

profile of v5, /device:TPU:6, one launch (start us, length us, event | category | flops | bytes accessed | tf_op | source)
XLA Modules:
  0.0 99.6 jit_solution(5491887566255028184)
XLA Ops:
  0.6 97.6 %shard_map.93 = (bf16[64,4096]{1,0:T(8,128)(2,1)S(1)}, bf16[64,4096]{1,0:T(8,128)(2,1)S(1)}, bf16[64,4096]{1,0:T(8,128)(2,1)S(1)}, bf16[64,4096]{1,0:T(8,128)(2,1)S(1)}) custom-call(bf16[64,4096]{1,0:T(8,128)(2,1)} %q_in.1, bf16[64,4096]{1,0:T(8,128)(2,1)} %k_in.1, bf16[64,4096]{1,0:T(8,128)(2,1)} %v_in.1, bf16[64,4096]{1,0:T(8,128)(2,1)} %g_in.1, ...), custom_call_target="tpu_custom_call" | custom-call | tf_op jit(solution)/shard_map/pallas_call | solution.py:401
  98.2 1.4 %shard_map.94 = (bf16[64,4096]{1,0:T(8,128)(2,1)}, bf16[64,4096]{1,0:T(8,128)(2,1)}, bf16[64,4096]{1,0:T(8,128)(2,1)}, bf16[64,4096]{1,0:T(8,128)(2,1)}) custom-call(bf16[64,4096]{1,0:T(8,128)(2,1)S(1)} %get-tuple-element.8.a_in, bf16[64,4096]{1,0:T(8,128)(2,1)S(1)} %get-tuple-element.9.b_in, bf16[64,4096]{1,0:T(8,128)(2,1)S(1)} %get-tuple-element.10.c_in, ...), custom_call_target="tpu_custom_call" | custom-call | tf_op jit(solution)/shard_map/pallas_call | solution.py:438

commit v6 on v5

--- a/solution.py
+++ b/solution.py
@@ -256,10 +256,10 @@
         attn = (acc * inv).astype(BF).astype(F32)
         stage[h, 0] = attn.T.astype(BF)
         grad_t = qg[h, 1].astype(F32).T
-        dot_row = jnp.sum(grad_t * attn, axis=0, keepdims=True) * inv
         grad_ts = grad_t * inv
         grad_tb = grad_ts.astype(BF)
         grad_b = grad_ts.T.astype(BF)
+        dot_row = jnp.sum(grad_tb.astype(F32) * attn, axis=0, keepdims=True)
         acc = jnp.zeros((HD, group), F32)
         for i, (place, keys, vals) in enumerate(spans):
             eb = ebuf[place, :]

time: 100 us -> 100 us (level)
  no operation moved by 1% of the time
where the time goes in v6:
time: 100 us; the launch traced here: 99.6 us
  Pallas kernels  99 us (99%)
    pallas_call x1, Pallas kernels, per_device(): pl.pallas_call(functools.partial(kernel, cfg), out_shape=[jax.ShapeDtypeS...  97.6 us

profile of v6, /device:TPU:6, one launch (start us, length us, event | category | flops | bytes accessed | tf_op | source)
XLA Modules:
  0.0 99.6 jit_solution(4273104741463902524)
XLA Ops:
  0.6 97.6 %shard_map.93 = (bf16[64,4096]{1,0:T(8,128)(2,1)S(1)}, bf16[64,4096]{1,0:T(8,128)(2,1)S(1)}, bf16[64,4096]{1,0:T(8,128)(2,1)S(1)}, bf16[64,4096]{1,0:T(8,128)(2,1)S(1)}) custom-call(bf16[64,4096]{1,0:T(8,128)(2,1)} %q_in.1, bf16[64,4096]{1,0:T(8,128)(2,1)} %k_in.1, bf16[64,4096]{1,0:T(8,128)(2,1)} %v_in.1, bf16[64,4096]{1,0:T(8,128)(2,1)} %g_in.1, ...), custom_call_target="tpu_custom_call" | custom-call | tf_op jit(solution)/shard_map/pallas_call | solution.py:401
  98.2 1.4 %shard_map.94 = (bf16[64,4096]{1,0:T(8,128)(2,1)}, bf16[64,4096]{1,0:T(8,128)(2,1)}, bf16[64,4096]{1,0:T(8,128)(2,1)}, bf16[64,4096]{1,0:T(8,128)(2,1)}) custom-call(bf16[64,4096]{1,0:T(8,128)(2,1)S(1)} %get-tuple-element.8.a_in, bf16[64,4096]{1,0:T(8,128)(2,1)S(1)} %get-tuple-element.9.b_in, bf16[64,4096]{1,0:T(8,128)(2,1)S(1)} %get-tuple-element.10.c_in, ...), custom_call_target="tpu_custom_call" | custom-call | tf_op jit(solution)/shard_map/pallas_call | solution.py:438
